TPU v7x, 32 devices: a whole 2x2x4 slice. The times are simulated.
32 devices in a mesh: dp: 8 (over z, x), mp: 4 (over y, core).
Axes of the slice: x: 2, y: 2, z: 4, core: 2. Of those that a mesh axis runs over, the one named last changes fastest.
Arguments:
- features: bfloat16 [8192, 1024], P('dp'), may hold values from -6 to 6
- out_grads: bfloat16 [8192, 4, 1024], P('dp', None, 'mp'), may hold values from -0.0625 to 0.0625
- norm_grads: float32 [8, 2048], P('dp'), may hold values from -2 to 2
- owners: int32 [5], replicated, may hold values from 0 to 7, as said below
- moment1: float32 [4, 1024, 1024], P(None, 'dp', 'mp'), may hold values from -6 to 6
- moment2: float32 [4, 1024, 1024], P(None, 'dp', 'mp'), may hold values from 0.1 to 10
- left_stats: float32 [4, 1024, 1024], P(None, 'dp', 'mp'), may hold values from -1024 to 1024, as said below
- right_stats: float32 [4, 1024, 1024], P(None, 'dp', 'mp'), may hold values from -1024 to 1024, as said below
- left_basis: float32 [4, 1024, 1024], P(None, 'dp', 'mp'), may hold values from -1 to 2
- right_basis: float32 [4, 1024, 1024], P(None, 'dp', 'mp'), may hold values from -1 to 2
- norm_m: float32 [2048], P('dp'), may hold values from -6 to 6
- norm_v: float32 [2048], P('dp'), may hold values from 0.1 to 10
Outputs:
- new_moment1: float32 [4, 1024, 1024], P(None, 'dp', 'mp')
- new_moment2: float32 [4, 1024, 1024], P(None, 'dp', 'mp')
- new_left_stats: float32 [4, 1024, 1024], P(None, 'dp', 'mp')
- new_right_stats: float32 [4, 1024, 1024], P(None, 'dp', 'mp')
- new_left_basis: float32 [4, 1024, 1024], P(None, 'dp', 'mp')
- new_right_basis: float32 [4, 1024, 1024], P(None, 'dp', 'mp')
- update_slots: bfloat16 [8, 1024, 1024], P('dp', None, 'mp')
- new_norm_m: float32 [2048], P('dp')
- new_norm_v: float32 [2048], P('dp')
- norm_slots: float32 [8, 2048], P('dp')
Inputs may be any that keep to these rules, and one draw needn't show every extreme that they name: `owners`: the first 4 entries are distinct, so a dp index owns at most one tile; the last entry may equal any of them. `left_stats`: each tile of statistics is symmetric. `right_stats`: each tile of statistics is symmetric.
All inputs are finite; a program needn't handle non-finite values.
Results may differ from a plain program's by a relative error of at most 0.0072.
Values may be sent and summed in bfloat16 or wider, within the bound.
A program may use at most 128 MiB of HBM per device.

v0:
```python
import jax
import jax.numpy as jnp
from jax import lax
from jax.sharding import PartitionSpec as P

FIX_ONE = 1.0 - 0.9**10
FIX_TWO = 1.0 - 0.95**10
BF = jnp.bfloat16
F32 = jnp.float32


def contract(left, right, left_dim, right_dim):
    return lax.dot_general(
        left, right, (((left_dim,), (right_dim,)), ((), ())), preferred_element_type=F32
    )


def to_tile(blocks):
    out = lax.all_to_all(blocks, "mp", split_axis=1, concat_axis=1, tiled=True)
    k, n, r, c = out.shape
    return out.transpose(0, 2, 1, 3).reshape(k, r, n * c)


def to_home(rows, n):
    k, r, c = rows.shape
    out = rows.reshape(k, r, n, c // n).transpose(0, 2, 1, 3)
    return lax.all_to_all(out, "mp", split_axis=1, concat_axis=1, tiled=True)


def gather_rows(rows):
    return lax.all_gather(rows, "dp", axis=0, tiled=True)


def normalize(power):
    wide = power.astype(F32)
    return lax.rsqrt(jnp.sum(wide * wide, axis=0, keepdims=True) + 1e-06)


def shards(
    features,
    out_grads,
    norm_grads,
    owners,
    moment1,
    moment2,
    left_stats,
    right_stats,
    left_basis,
    right_basis,
    norm_m,
    norm_v,
):
    dp = lax.axis_size("dp")
    tiles, slab, width = moment1.shape
    full = slab * dp
    me = lax.axis_index("dp")
    row0 = me * slab
    narrow = to_tile(jnp.stack([left_basis, right_basis, left_stats, right_stats]).astype(BF))
    left_full = gather_rows(narrow[0])
    right_full = gather_rows(narrow[1])
    flat = out_grads.reshape(out_grads.shape[0], tiles * width)
    partial = contract(features, flat, 0, 0).astype(BF).reshape(dp, slab, tiles * width)
    parts = lax.all_to_all(partial, "dp", split_axis=0, concat_axis=0, tiled=True)
    grad_home = jnp.sum(parts.astype(F32), axis=0).astype(BF)
    grad_home = grad_home.reshape(slab, tiles, width).transpose(1, 0, 2)
    grad_rows = to_tile(grad_home[None])[0]
    grad_full = gather_rows(grad_rows)
    wide = to_tile(jnp.stack([moment1, moment2]))
    prod_l = contract(grad_rows, grad_full, 1, 1)
    grad_cols = lax.dynamic_slice_in_dim(grad_full, row0, slab, 1)
    prod_r = contract(grad_cols, grad_full, 0, 0)
    stats_l = (0.95 * narrow[2].astype(F32) + 0.05 * prod_l).astype(BF)
    stats_r = (0.95 * narrow[3].astype(F32) + 0.05 * prod_r).astype(BF)
    power_l = contract(stats_l, left_full, 1, 0).astype(BF)
    power_r = contract(stats_r, right_full, 1, 0).astype(BF)
    power_l_full = gather_rows(power_l)
    power_r_full = gather_rows(power_r)
    left_cols = lax.dynamic_slice_in_dim(left_full, row0, slab, 1)
    half = contract(left_cols, grad_full, 0, 0).astype(BF)
    rotated = contract(half, right_full, 1, 0)
    tile_one = 0.9 * wide[0] + 0.1 * rotated
    tile_two = 0.95 * wide[1] + 0.05 * rotated * rotated
    direction = (tile_one / FIX_ONE / (jnp.sqrt(tile_two / FIX_TWO) + 1e-08)).astype(BF)
    back = contract(direction, right_full, 1, 1).astype(BF)
    back_full = gather_rows(back)
    home1 = to_home(jnp.stack([rotated, prod_l, prod_r]).astype(BF), tiles).astype(F32)
    new_one = 0.9 * moment1 + 0.1 * home1[0]
    new_two = 0.95 * moment2 + 0.05 * home1[0] * home1[0]
    new_sl = 0.95 * left_stats + 0.05 * home1[1]
    new_sr = 0.95 * right_stats + 0.05 * home1[2]
    update = contract(narrow[0], back_full, 1, 0).astype(BF)

    def refine(power_full, power_rows):
        scale = normalize(power_full)
        iter_full = (power_full.astype(F32) * scale).astype(BF)
        iter_rows = (power_rows.astype(F32) * scale).astype(BF)
        gram = contract(iter_rows, iter_full, 1, 1).astype(BF)
        return 1.5 * iter_rows.astype(F32) - 0.5 * contract(gram, iter_full, 1, 0)

    new_l = refine(power_l_full, power_l)
    new_r = refine(power_r_full, power_r)
    home2 = to_home(jnp.stack([new_l.astype(BF), new_r.astype(BF), update]), tiles)
    new_bl = home2[0].astype(F32)
    new_br = home2[1].astype(F32)
    slot_of = jnp.arange(dp, dtype=jnp.int32)[:, None, None]
    slots = jnp.zeros((dp, slab, width), BF)
    for n in range(tiles):
        slots = jnp.where(slot_of == owners[n], home2[2, n][None], slots)
    update_slot = lax.all_to_all(slots, "dp", split_axis=0, concat_axis=0, tiled=True)
    update_slot = update_slot.reshape(1, full, width)
    norm_parts = norm_grads.reshape(dp, norm_m.shape[0])
    norm_parts = lax.all_to_all(norm_parts, "dp", split_axis=0, concat_axis=0, tiled=True)
    norm_total = jnp.sum(norm_parts, axis=0)
    new_nm = 0.9 * norm_m + 0.1 * norm_total
    new_nv = 0.95 * norm_v + 0.05 * norm_total * norm_total
    norm_step = new_nm / FIX_ONE / (jnp.sqrt(new_nv / FIX_TWO) + 1e-08)
    to_owner = (jnp.arange(dp, dtype=jnp.int32) == owners[tiles])[:, None]
    norm_out = jnp.where(to_owner, norm_step[None], 0.0)
    norm_slot = lax.all_to_all(norm_out, "dp", split_axis=0, concat_axis=0, tiled=True)
    norm_slot = norm_slot.reshape(1, -1)
    return (
        new_one,
        new_two,
        new_sl,
        new_sr,
        new_bl,
        new_br,
        update_slot,
        new_nm,
        new_nv,
        norm_slot,
    )


def solution(mesh):
    in_specs = (
        P("dp", None),
        P("dp", None, "mp"),
        P("dp", None),
        P(),
        P(None, "dp", "mp"),
        P(None, "dp", "mp"),
        P(None, "dp", "mp"),
        P(None, "dp", "mp"),
        P(None, "dp", "mp"),
        P(None, "dp", "mp"),
        P("dp"),
        P("dp"),
    )
    out_specs = (
        P(None, "dp", "mp"),
        P(None, "dp", "mp"),
        P(None, "dp", "mp"),
        P(None, "dp", "mp"),
        P(None, "dp", "mp"),
        P(None, "dp", "mp"),
        P("dp", None, "mp"),
        P("dp"),
        P("dp"),
        P("dp", None),
    )
    return jax.shard_map(shards, mesh=mesh, in_specs=in_specs, out_specs=out_specs, check_vma=False)
```

profile of v0, /device:TPU:0, one launch (start us, length us, event | category | flops | bytes accessed | tf_op | source)
XLA Modules:
  0.0 443.4 jit_solution(10692234722072050169)
XLA Ops:
  7.2 2.2 copy.122
  9.5 2.4 convolution_convert_fusion
  11.9 55.4 %all_to_all.50 = bf16[8,128,1024]{2,1,0:T(8,128)(2,1)} all-to-all(bf16[8,128,1024]{2,1,0:T(8,128)(2,1)S(1)} %bitcast.115), channel_id=1, replica_groups=mesh['dp'=8,'mp'=4] {'dp'}, dimensions={0} | all-to-all | bytes 4194304 | tf_op jit(solution)/shard_map/all_to_all | solution.py:63
  67.3 2.0 reduce_sum.39
  69.4 0.8 copy.97
  70.2 1.1 copy.98
  71.3 9.1 %all_to_all.51 = bf16[1,4,128,256]{3,2,0,1:T(8,128)(2,1)} all-to-all(bf16[1,4,128,256]{3,2,0,1:T(8,128)(2,1)S(1)} %copy.98), channel_id=1, replica_groups=mesh['dp'=8,'mp'=4] {'mp'}, dimensions={1} | all-to-all | bytes 524288 | tf_op jit(solution)/shard_map/all_to_all | solution.py:19
  80.4 1.8 copy.99
  82.6 1.2 copy.93
  83.8 1.2 copy.92
  85.2 16.9 %all_to_all.52 = bf16[4,4,128,256]{2,3,0,1:T(8,128)(2,1)S(1)} all-to-all(bf16[4,4,128,256]{2,3,0,1:T(8,128)(2,1)S(1)} %pad_maximum_fusion), channel_id=1, replica_groups=mesh['dp'=8,'mp'=4] {'mp'}, dimensions={1} | all-to-all | bytes 2097152 | tf_op jit(solution)/shard_map/all_to_all | solution.py:19
  102.1 0.8 fusion.83
  103.0 0.7 all-gather.7.cloned.1.call-update
  103.8 1.1 convert_multiply_fusion.5
  104.8 1.2 copy.117
  106.1 24.6 %all-gather.9.cloned.1.call-done = bf16[1024,1024]{0,1:T(8,128)(2,1)} async-done(((bf16[128,1024]{0,1:T(8,128)(2,1)}), bf16[1024,1024]{0,1:T(8,128)(2,1)}) %all-gather.9.cloned.1.call-update) | async-done | bytes 2097168 | tf_op jit(solution)/shard_map/all_gather | solution.py:31
  130.7 3.4 fusion.85
  134.1 47.8 %all-gather.11.cloned.1.call-done = bf16[1024,1024]{0,1:T(8,128)(2,1)} async-done(((bf16[128,1024]{0,1:T(8,128)(2,1)}), bf16[1024,1024]{0,1:T(8,128)(2,1)}) %all-gather.11.cloned.1.call-update) | async-done | bytes 2097168 | tf_op jit(solution)/shard_map/all_gather | solution.py:31
  181.8 3.3 convolution_convert_fusion.3
  185.3 0.2 copy.116
  185.5 2.8 fusion.86
  188.2 44.8 %all-gather.7.cloned.1.call-done = bf16[1024,1024]{0,1:T(8,128)(2,1)} async-done(((bf16[128,1024]{0,1:T(8,128)(2,1)}), bf16[1024,1024]{0,1:T(8,128)(2,1)}) %all-gather.7.cloned.1.call-update) | async-done | bytes 2097168 | tf_op jit(solution)/shard_map/all_gather | solution.py:31
  233.0 3.1 convolution_convert_fusion.4
  236.2 1.2 copy.108
  237.4 1.2 copy.109
  238.8 17.0 %all_to_all.53 = f32[2,4,128,256]{2,3,0,1:T(8,128)S(1)} all-to-all(f32[2,4,128,256]{2,3,0,1:T(8,128)S(1)} %pad_maximum_fusion.1), channel_id=1, replica_groups=mesh['dp'=8,'mp'=4] {'mp'}, dimensions={1} | all-to-all | bytes 2097152 | tf_op jit(solution)/shard_map/all_to_all | solution.py:19
  255.9 1.0 copy.118
  257.1 4.8 %fusion.87 = (bf16[128,1024]{1,0:T(8,128)(2,1)}, f32[128,1024]{1,0:T(8,128)}) fusion(bf16[1024,1024]{0,1:T(8,128)(2,1)} %all-gather.11.cloned.1.call-done, bf16[1024,1024]{0,1:T(8,128)(2,1)} %all-gather.9.cloned.1.call-done, bf16[1024,1024]{0,1:T(8,128)(2,1)} %all-gather.7.cloned.1.call-done, s32[]{:T(128)S(6)} %select_n.28), kind=kOutput, calls=%fused_computation.109 | convolution fusion | flops 537133056 | bytes 5242884 | tf_op jit(solution)/shard_map/dot_general | solution.py:13
  261.9 3.1 convolution_convert_fusion.2
  265.1 3.5 all-to-all-start.7
  268.6 0.7 fusion.84
  269.3 0.7 iota_compare_fusion
  269.9 5.2 %all-to-all-done.7 = f32[8,1,256]{2,1,0:T(1,128)S(1)} async-done(((f32[8,1,256]{2,1,0:T(1,128)}), f32[8,1,256]{2,1,0:T(1,128)S(1)}, u32[]{:S(2)}, u32[]{:S(2)}) %all-to-all-start.7) | async-done | bytes 8224 | tf_op jit(solution)/shard_map/all_to_all | solution.py:112
  275.2 0.6 add_divide_fusion
  275.8 0.7 broadcast_select_fusion
  276.4 3.5 all-to-all-start.8
  280.0 3.1 all-gather.15.cloned.1.call-done
  283.1 2.1 fusion.2
  285.1 3.5 fusion.24
  288.9 43.8 %all-gather.13.cloned.1.call-done = bf16[1024,1024]{1,0:T(8,128)(2,1)} async-done(((bf16[128,1024]{1,0:T(8,128)(2,1)}), bf16[1024,1024]{1,0:T(8,128)(2,1)}) %all-gather.13.cloned.1.call-update) | async-done | bytes 2097168 | tf_op jit(solution)/shard_map/all_gather | solution.py:31
  332.7 2.1 fusion
  334.8 3.5 fusion.27
  338.5 44.4 %all-gather.17.cloned.1.call-done = bf16[1024,1024]{1,0:T(8,128)(2,1)} async-done(((bf16[128,1024]{1,0:T(8,128)(2,1)}), bf16[1024,1024]{1,0:T(8,128)(2,1)}) %all-gather.17.cloned.1.call-update) | async-done | bytes 2097168 | tf_op jit(solution)/shard_map/all_gather | solution.py:31
  382.9 2.1 convolution_convert_fusion.1
  385.2 1.0 maximum_bitcast_fusion.1
  386.2 3.6 all-to-all-start.5
  389.8 1.8 stack.58
  391.6 1.7 copy.100
  393.3 0.9 stack.60
  394.2 1.7 copy.102
  396.1 2.0 maximum_bitcast_fusion
  398.1 3.3 all-to-all-done.5
  401.4 4.2 all-to-all-start.3
  405.6 1.3 iota_compare_fusion.1
  406.9 1.2 iota_compare_fusion.3
  408.1 1.1 select_select_fusion
  409.2 8.1 %all-to-all-done.3 = bf16[3,4,128,256]{3,2,0,1:T(8,128)(2,1)} async-done(((bf16[3,4,128,256]{3,2,0,1:T(8,128)(2,1)}), bf16[3,4,128,256]{3,2,0,1:T(8,128)(2,1)}, u32[]{:S(2)}, u32[]{:S(2)}) %all-to-all-start.3) | async-done | bytes 786464 | tf_op jit(solution)/shard_map/all_to_all | solution.py:27
  417.3 3.5 all-to-all-start.6
  420.8 1.4 convert_element_type.101
  422.5 1.5 fusion.48
  424.0 1.1 fusion.54
  425.1 10.1 %all-to-all-done.6 = bf16[8,128,256]{2,1,0:T(8,128)(2,1)S(1)} async-done(((bf16[8,128,256]{2,1,0:T(8,128)(2,1)}), bf16[8,128,256]{2,1,0:T(8,128)(2,1)S(1)}, u32[]{:S(2)}, u32[]{:S(2)}) %all-to-all-start.6) | async-done | bytes 524320 | tf_op jit(solution)/shard_map/all_to_all | solution.py:109
  435.1 0.8 copy.129
  435.9 0.6 copy.130
  (68 shorter events, 2.6 us)
Async XLA Ops:
  7.2 2.3 copy-start
  7.2 123.5 %all-gather.9.cloned.1.call-start = ((), (), s32[]{:S(2)}) async-start(), calls=%async_computation.10 | async-start | bytes 2359296 | tf_op jit(solution)/shard_map/all_gather | solution.py:31
  67.3 14.9 %copy-start.4 = (f32[4,128,256]{2,1,0:T(8,128)S(1)}, f32[4,128,256]{2,1,0:T(8,128)}, u32[]{:S(2)}) copy-start(f32[4,128,256]{2,1,0:T(8,128)} %param.19) | copy-start | bytes 1572868
  69.3 13.1 %copy-start.6 = (f32[4,128,256]{2,1,0:T(8,128)S(1)}, f32[4,128,256]{2,1,0:T(8,128)}, u32[]{:S(2)}) copy-start(f32[4,128,256]{2,1,0:T(8,128)} %param.18) | copy-start | bytes 1572868
  82.2 99.7 %all-gather.11.cloned.1.call-start = ((), (), s32[]{:S(2)}) async-start(), calls=%async_computation.11 | async-start | bytes 2359296 | tf_op jit(solution)/shard_map/all_gather | solution.py:31
  103.0 130.1 %all-gather.7.cloned.1.call-start = ((), (), s32[]{:S(2)}) async-start(), calls=%async_computation.9 | async-start | bytes 2359296 | tf_op jit(solution)/shard_map/all_gather | solution.py:31
  103.7 179.4 %all-gather.15.cloned.1.call-start = ((), (), s32[]{:S(2)}) async-start(), calls=%async_computation.13 | async-start | bytes 2359296 | tf_op jit(solution)/shard_map/all_gather | solution.py:31
  134.0 51.2 %copy-start.3 = (f32[1,128,4,256]{1,3,2,0:T(8,128)S(1)}, f32[1,128,4,256]{1,3,2,0:T(8,128)}, u32[]{:S(2)}) copy-start(f32[1,128,4,256]{1,3,2,0:T(8,128)} %get-tuple-element.17) | copy-start | bytes 1572868
  181.8 3.6 copy-start.1
  185.2 147.5 %all-gather.13.cloned.1.call-start = ((), (), s32[]{:S(2)}) async-start(), calls=%async_computation.12 | async-start | bytes 2359296 | tf_op jit(solution)/shard_map/all_gather | solution.py:31
  236.2 146.7 %all-gather.17.cloned.1.call-start = ((), (), s32[]{:S(2)}) async-start(), calls=%async_computation.14 | async-start | bytes 2359296 | tf_op jit(solution)/shard_map/all_gather | solution.py:31
  257.1 4.8 %copy-start.14 = (f32[128,1024]{1,0:T(8,128)S(1)}, f32[128,1024]{1,0:T(8,128)}, u32[]{:S(2)}) copy-start(f32[128,1024]{1,0:T(8,128)} %copy.118) | copy-start | bytes 1572868
  261.9 6.7 %copy-start.15 = (s32[5]{0:T(128)S(1)}, s32[5]{0:T(128)}, u32[]{:S(2)}) copy-start(s32[5]{0:T(128)} %param.15) | copy-start | bytes 64
  261.9 13.3 %copy-start.16 = (f32[256]{0:T(256)S(1)}, f32[256]{0:T(256)}, u32[]{:S(2)}) copy-start(f32[256]{0:T(256)} %param.23) | copy-start | bytes 3076
  261.9 13.3 %copy-start.17 = (f32[256]{0:T(256)S(1)}, f32[256]{0:T(256)}, u32[]{:S(2)}) copy-start(f32[256]{0:T(256)} %param.22) | copy-start | bytes 3076
  265.1 20.1 %copy-start.12 = (bf16[128,1024]{1,0:T(8,128)(2,1)S(1)}, bf16[128,1024]{1,0:T(8,128)(2,1)}, u32[]{:S(2)}) copy-start(bf16[128,1024]{1,0:T(8,128)(2,1)} %convolution_convert_fusion.3) | copy-start | bytes 786436
  265.1 10.1 %all-to-all-start.7 = ((f32[8,1,256]{2,1,0:T(1,128)}), f32[8,1,256]{2,1,0:T(1,128)S(1)}, u32[]{:S(2)}, u32[]{:S(2)}) async-start(f32[8,1,256]{2,1,0:T(1,128)} %bitcast.38), calls=%async_computation.7 | async-start | bytes 16384 | tf_op jit(solution)/shard_map/all_to_all | solution.py:112
  276.4 109.7 %all-to-all-start.8 = ((f32[8,1,256]{2,1,0:T(1,128)}), f32[8,1,256]{2,1,0:T(1,128)S(1)}, u32[]{:S(2)}, u32[]{:S(2)}) async-start(f32[8,1,256]{2,1,0:T(1,128)} %broadcast_select_fusion), calls=%async_computation.8 | async-start | bytes 16384 | tf_op jit(solution)/shard_map/all_to_all | solution.py:119
  288.6 46.1 %copy-start.13 = (bf16[128,1024]{1,0:T(8,128)(2,1)S(1)}, bf16[128,1024]{1,0:T(8,128)(2,1)}, u32[]{:S(2)}) copy-start(bf16[128,1024]{1,0:T(8,128)(2,1)} %convolution_convert_fusion.4) | copy-start | bytes 786436
  334.7 48.1 %copy-start.2 = (bf16[1,128,4,256]{1,3,2,0:T(8,128)(2,1)S(1)}, bf16[1,128,4,256]{1,3,2,0:T(8,128)(2,1)}, u32[]{:S(2)}) copy-start(bf16[1,128,4,256]{1,3,2,0:T(8,128)(2,1)} %get-tuple-element.21) | copy-start | bytes 786436
  385.2 8.2 %copy-start.10 = (bf16[128,1024]{1,0:T(8,128)(2,1)S(1)}, bf16[128,1024]{1,0:T(8,128)(2,1)}, u32[]{:S(2)}) copy-start(bf16[128,1024]{1,0:T(8,128)(2,1)} %get-tuple-element.34) | copy-start | bytes 786436
  386.2 9.7 %copy-start.11 = (bf16[128,1024]{1,0:T(8,128)(2,1)S(1)}, bf16[128,1024]{1,0:T(8,128)(2,1)}, u32[]{:S(2)}) copy-start(bf16[128,1024]{1,0:T(8,128)(2,1)} %get-tuple-element.36) | copy-start | bytes 786436
  386.2 15.2 %all-to-all-start.5 = ((bf16[3,4,128,256]{3,2,0,1:T(8,128)(2,1)}), bf16[3,4,128,256]{3,2,0,1:T(8,128)(2,1)S(1)}, u32[]{:S(2)}, u32[]{:S(2)}) async-start(bf16[3,4,128,256]{3,2,0,1:T(8,128)(2,1)} %maximum_bitcast_fusion.1), calls=%async_computation.5 | async-start | bytes 1572864 | tf_op jit(solution)/shard_map/all_to_all | solution.py:27
  401.4 15.9 %all-to-all-start.3 = ((bf16[3,4,128,256]{3,2,0,1:T(8,128)(2,1)}), bf16[3,4,128,256]{3,2,0,1:T(8,128)(2,1)}, u32[]{:S(2)}, u32[]{:S(2)}) async-start(bf16[3,4,128,256]{3,2,0,1:T(8,128)(2,1)} %maximum_bitcast_fusion), calls=%async_computation.3 | async-start | bytes 1572864 | tf_op jit(solution)/shard_map/all_to_all | solution.py:27
  417.3 17.9 %all-to-all-start.6 = ((bf16[8,128,256]{2,1,0:T(8,128)(2,1)}), bf16[8,128,256]{2,1,0:T(8,128)(2,1)S(1)}, u32[]{:S(2)}, u32[]{:S(2)}) async-start(bf16[8,128,256]{2,1,0:T(8,128)(2,1)} %select_select_fusion), calls=%async_computation.6 | async-start | bytes 1048576 | tf_op jit(solution)/shard_map/all_to_all | solution.py:109
  420.8 1.5 copy-start.5
  420.8 1.5 copy-start.7
  420.8 1.6 copy-start.8
  420.8 1.7 copy-start.9
Sparse Core Ops, SparseCore 0:
  82.3 48.3 all-gather.8
  133.3 48.5 all-gather.10
  184.5 48.5 all-gather.6
  235.6 47.4 all-gather.14
  285.0 47.5 all-gather.12
  335.2 47.6 all-gather.16
where the time goes:
time: 445 us; the launch traced here: 443 us
  waiting for transfers between devices  236 us (53%)
  blocking collectives  98.3 us (22%)
  matrix products  32 us (7%)
  local copies, waits for them, and re-layouts  24.2 us (5%)
  other arithmetic  20 us (4%)
  starting transfers between devices  18.5 us (4%)
  between operations  14.6 us (3%)
    all_gather x6, waiting for transfers between devices, gather_rows(): return lax.all_gather(rows, 'dp', axis=0, tiled=True)  208 us
    all_to_all x1, blocking collectives, shards(): lax.all_to_all(partial, 'dp', split_axis=0, concat_axis=0, tiled=True)  55.4 us
    all_to_all x3, blocking collectives, to_tile(): out = lax.all_to_all(blocks, 'mp', split_axis=1, concat_axis=1, tiled=True)  42.9 us
    dot_general x10, matrix products, contract(): lax.dot_general(left, right, (((left_dim,), (right_dim,)), ((), ())), pre...  32 us
    all_to_all x2, waiting for transfers between devices, to_home(): return lax.all_to_all(out, 'mp', split_axis=1, concat_axis=1, tiled=True)  11.3 us
    all_to_all x1, waiting for transfers between devices, shards(): lax.all_to_all(slots, 'dp', split_axis=0, concat_axis=0, tiled=True)  10.1 us
    unnamed x45, local copies, waits for them, and re-layouts  9.22 us
  transfers between devices with their start and end apart: 11, of which 10 were waited for; matrix products, arithmetic and copies ran while one was open for 14% of the time, Pallas kernels for 0%

commit v1 on v0

--- a/solution.py
+++ b/solution.py
@@ -28,7 +28,9 @@
 
 
 def gather_rows(rows):
-    return lax.all_gather(rows, "dp", axis=0, tiled=True)
+    return jnp.concatenate(
+        lax.all_to_all(jnp.stack([rows] * lax.axis_size("dp")), "dp", 0, 0), axis=0
+    )
 
 
 def normalize(power):

time: 445 us -> 511 us (1.15)
  waiting for transfers between devices: 236 us -> 354 us
  blocking collectives: 98.3 us -> 0 us
  starting transfers between devices: 18.5 us -> 64.1 us
  local copies, waits for them, and re-layouts: 24.2 us -> 41.7 us
  between operations: 14.6 us -> 1.08 us
  matrix products: 32 us -> 23.2 us
  other arithmetic: 20 us -> 25.4 us
    all_to_all x0 -> x10, waiting for transfers between devices: none -> 326 us  [the longest x6 256 us: gather_rows(): lax.all_to_all(jnp.stack([rows] * lax.axis_size('dp')), 'dp', 0, 0)]
    all_gather x6 -> x0, waiting for transfers between devices: 208 us -> none  [gather_rows(): return lax.all_gather(rows, 'dp', axis=0, tiled=True)]
    all_to_all x4 -> x0, blocking collectives: 98.3 us -> none  [the longest x1 55.4 us: shards(): lax.all_to_all(partial, 'dp', split_axis=0, concat_axis=0, tiled=True)]
    all_to_all x0 -> x10, starting transfers between devices: none -> 43.7 us  [the longest x6 25.3 us: gather_rows(): lax.all_to_all(jnp.stack([rows] * lax.axis_size('dp')), 'dp', 0, 0)]
    another operation x0 -> x7, local copies, waits for them, and re-layouts: none -> 12.8 us  [gather_rows(): jnp.stack([rows] * lax.axis_size('dp'))]
    dot_general x10, matrix products: 32 us -> 23.2 us  [contract(): lax.dot_general(left, right, (((left_dim,), (right_dim,)), ((), ())), pre...]
    all_to_all x2, waiting for transfers between devices: 11.3 us -> 17.9 us  [to_home(): return lax.all_to_all(out, 'mp', split_axis=1, concat_axis=1, tiled=True)]
    another operation x6, local copies, waits for them, and re-layouts: 6.29 us -> 0.63 us  [shards(): jnp.stack([rotated, prod_l, prod_r]).astype(BF)]
  transfers between devices with their start and end apart: 11 -> 15, of which waited for: 10 -> 13; matrix products, arithmetic and copies ran while one was open for 14% -> 13% of each run, Pallas kernels for 0% -> 0%
where the time goes in v1:
time: 511 us; the launch traced here: 509 us
  waiting for transfers between devices  354 us (69%)
  starting transfers between devices  64.1 us (13%)
  local copies, waits for them, and re-layouts  41.7 us (8%)
  other arithmetic  25.4 us (5%)
  matrix products  23.2 us (5%)
    all_to_all x6, waiting for transfers between devices, gather_rows(): lax.all_to_all(jnp.stack([rows] * lax.axis_size('dp')), 'dp', 0, 0)  256 us
    all_to_all x1, waiting for transfers between devices, shards(): lax.all_to_all(partial, 'dp', split_axis=0, concat_axis=0, tiled=True)  44.4 us
    all_to_all x3, waiting for transfers between devices, to_tile(): out = lax.all_to_all(blocks, 'mp', split_axis=1, concat_axis=1, tiled=True)  25.5 us
    all_to_all x6, starting transfers between devices, gather_rows(): lax.all_to_all(jnp.stack([rows] * lax.axis_size('dp')), 'dp', 0, 0)  25.3 us
    dot_general x10, matrix products, contract(): lax.dot_general(left, right, (((left_dim,), (right_dim,)), ((), ())), pre...  23.2 us
    all_to_all x2, waiting for transfers between devices, to_home(): return lax.all_to_all(out, 'mp', split_axis=1, concat_axis=1, tiled=True)  17.9 us
    unnamed x45, local copies, waits for them, and re-layouts  13.1 us
    another operation x7, local copies, waits for them, and re-layouts, gather_rows(): jnp.stack([rows] * lax.axis_size('dp'))  12.8 us
  transfers between devices with their start and end apart: 15, of which 13 were waited for; matrix products, arithmetic and copies ran while one was open for 13% of the time, Pallas kernels for 0%

profile of v1, /device:TPU:0, one launch (start us, length us, event | category | flops | bytes accessed | tf_op | source)
XLA Modules:
  0.0 509.4 jit_solution(16935816194279487394)
XLA Ops:
  0.7 1.4 copy.126
  2.0 1.2 copy.127
  3.3 1.2 copy.128
  5.3 2.0 pad_maximum_fusion
  7.4 4.3 all-to-all-start
  11.6 2.1 copy.159
  13.7 3.7 convolution_convert_fusion
  17.5 8.6 %all-to-all-done = bf16[4,4,128,256]{2,3,0,1:T(8,128)(2,1)S(1)} async-done(((bf16[4,4,128,256]{2,3,0,1:T(8,128)(2,1)}), bf16[4,4,128,256]{2,3,0,1:T(8,128)(2,1)S(1)}, u32[]{:S(2)}, u32[]{:S(2)}) %all-to-all-start) | async-done | bytes 1048608 | tf_op jit(solution)/shard_map/all_to_all | solution.py:19
  27.0 6.5 %all-to-all-start.2 = ((bf16[8,128,1024]{2,1,0:T(8,128)(2,1)}), bf16[8,128,1024]{2,1,0:T(8,128)(2,1)S(1)}, u32[]{:S(2)}, u32[]{:S(2)}) async-start(bf16[8,128,1024]{2,1,0:T(8,128)(2,1)} %bitcast.139), calls=%async_computation.2 | async-start | bytes 4194304 | tf_op jit(solution)/shard_map/all_to_all | solution.py:65
  33.6 1.2 copy.145
  34.8 1.2 copy.146
  37.1 44.4 %all-to-all-done.2 = bf16[8,128,1024]{2,1,0:T(8,128)(2,1)S(1)} async-done(((bf16[8,128,1024]{2,1,0:T(8,128)(2,1)}), bf16[8,128,1024]{2,1,0:T(8,128)(2,1)S(1)}, u32[]{:S(2)}, u32[]{:S(2)}) %all-to-all-start.2) | async-done | bytes 2097184 | tf_op jit(solution)/shard_map/all_to_all | solution.py:65
  81.5 4.3 all-to-all-start.9
  85.8 1.3 copy.163
  88.5 11.8 %all-to-all-done.9 = f32[2,4,128,256]{2,3,0,1:T(8,128)} async-done(((f32[2,4,128,256]{2,3,0,1:T(8,128)}), f32[2,4,128,256]{2,3,0,1:T(8,128)}, u32[]{:S(2)}, u32[]{:S(2)}) %all-to-all-start.9) | async-done | bytes 1048608 | tf_op jit(solution)/shard_map/all_to_all | solution.py:19
  100.3 3.4 all-to-all-start.3
  104.6 5.1 all-to-all-done.3
  109.6 1.6 stack.100
  111.3 3.6 all-to-all-start.1
  114.9 1.1 copy.136
  116.0 47.0 %all-to-all-done.1 = bf16[8,128,1024]{2,1,0:T(8,128)(2,1)S(1)} async-done(((bf16[8,128,1024]{2,1,0:T(8,128)(2,1)}), bf16[8,128,1024]{2,1,0:T(8,128)(2,1)S(1)}, u32[]{:S(2)}, u32[]{:S(2)}) %all-to-all-start.1) | async-done | bytes 2097184 | tf_op jit(solution)/shard_map/all_to_all | solution.py:32
  163.0 1.8 stack.102
  165.0 3.6 all-to-all-start.5
  168.6 1.1 copy.134
  170.6 46.4 %all-to-all-done.5 = bf16[8,128,1024]{2,1,0:T(8,128)(2,1)S(1)} async-done(((bf16[8,128,1024]{2,1,0:T(8,128)(2,1)}), bf16[8,128,1024]{2,1,0:T(8,128)(2,1)S(1)}, u32[]{:S(2)}, u32[]{:S(2)}) %all-to-all-start.5) | async-done | bytes 2097184 | tf_op jit(solution)/shard_map/all_to_all | solution.py:32
  217.0 2.7 stack.101
  219.7 3.6 all-to-all-start.4
  223.4 1.3 copy.162
  224.7 1.1 slice_multiply_fusion.1
  225.7 2.0 copy.155
  227.7 2.0 copy.156
  229.8 42.0 %all-to-all-done.4 = bf16[8,128,1024]{2,1,0:T(8,128)(2,1)S(1)} async-done(((bf16[8,128,1024]{2,1,0:T(8,128)(2,1)}), bf16[8,128,1024]{2,1,0:T(8,128)(2,1)S(1)}, u32[]{:S(2)}, u32[]{:S(2)}) %all-to-all-start.4) | async-done | bytes 2097184 | tf_op jit(solution)/shard_map/all_to_all | solution.py:32
  271.8 3.6 all-to-all-start.13
  275.4 3.4 fusion.53
  278.8 3.7 convolution_convert_fusion.2
  282.5 2.6 stack.114
  285.1 6.0 %all-to-all-start.10 = ((bf16[8,128,1024]{2,1,0:T(8,128)(2,1)}), bf16[8,128,1024]{2,1,0:T(8,128)(2,1)}, u32[]{:S(2)}, u32[]{:S(2)}) async-start(bf16[8,128,1024]{2,1,0:T(8,128)(2,1)} %stack.114), calls=%async_computation.10 | async-start | bytes 4194304 | tf_op jit(solution)/shard_map/all_to_all | solution.py:32
  292.2 1.2 copy.154
  293.4 1.2 fusion.51
  295.5 43.5 %all-to-all-done.10 = bf16[8,128,1024]{2,1,0:T(8,128)(2,1)} async-done(((bf16[8,128,1024]{2,1,0:T(8,128)(2,1)}), bf16[8,128,1024]{2,1,0:T(8,128)(2,1)}, u32[]{:S(2)}, u32[]{:S(2)}) %all-to-all-start.10) | async-done | bytes 2097184 | tf_op jit(solution)/shard_map/all_to_all | solution.py:32
  339.1 1.7 stack.109
  340.7 4.5 all-to-all-start.8
  348.4 44.7 %all-to-all-done.8 = bf16[8,128,1024]{2,1,0:T(8,128)(2,1)} async-done(((bf16[8,128,1024]{2,1,0:T(8,128)(2,1)}), bf16[8,128,1024]{2,1,0:T(8,128)(2,1)}, u32[]{:S(2)}, u32[]{:S(2)}) %all-to-all-start.8) | async-done | bytes 2097184 | tf_op jit(solution)/shard_map/all_to_all | solution.py:32
  393.0 1.6 stack.107
  394.6 3.9 all-to-all-start.7
  401.1 2.1 convolution_convert_fusion.1
  403.4 2.1 multiply_reduce_fusion
  405.5 3.5 fusion
  409.0 4.1 fusion.5
  413.1 1.1 stack.110
  414.3 32.6 %all-to-all-done.7 = bf16[8,128,1024]{2,1,0:T(8,128)(2,1)S(1)} async-done(((bf16[8,128,1024]{2,1,0:T(8,128)(2,1)}), bf16[8,128,1024]{2,1,0:T(8,128)(2,1)S(1)}, u32[]{:S(2)}, u32[]{:S(2)}) %all-to-all-start.7) | async-done | bytes 2097184 | tf_op jit(solution)/shard_map/all_to_all | solution.py:32
  446.9 3.6 all-to-all-start.14
  451.0 1.9 fusion.1
  452.9 3.4 fusion.4
  457.5 3.6 all-to-all-start.11
  462.8 9.9 %all-to-all-done.11 = bf16[3,4,128,256]{3,2,0,1:T(8,128)(2,1)S(1)} async-done(((bf16[3,4,128,256]{3,2,0,1:T(8,128)(2,1)}), bf16[3,4,128,256]{3,2,0,1:T(8,128)(2,1)S(1)}, u32[]{:S(2)}, u32[]{:S(2)}) %all-to-all-start.11) | async-done | bytes 786464 | tf_op jit(solution)/shard_map/all_to_all | solution.py:27
  472.7 3.5 all-to-all-start.6
  476.2 1.2 iota_compare_fusion.1
  477.4 1.3 iota_compare_fusion.3
  479.8 8.0 %all-to-all-done.6 = bf16[3,4,128,256]{3,2,0,1:T(8,128)(2,1)S(1)} async-done(((bf16[3,4,128,256]{3,2,0,1:T(8,128)(2,1)}), bf16[3,4,128,256]{3,2,0,1:T(8,128)(2,1)S(1)}, u32[]{:S(2)}, u32[]{:S(2)}) %all-to-all-start.6) | async-done | bytes 786464 | tf_op jit(solution)/shard_map/all_to_all | solution.py:27
  487.8 6.0 %all-to-all-start.12 = ((bf16[8,128,256]{2,1,0:T(8,128)(2,1)}), bf16[8,128,256]{2,1,0:T(8,128)(2,1)S(1)}, u32[]{:S(2)}, u32[]{:S(2)}) async-start(bf16[8,128,256]{2,1,0:T(8,128)(2,1)} %select_select_fusion), calls=%async_computation.12 | async-start | bytes 1048576 | tf_op jit(solution)/shard_map/all_to_all | solution.py:111
  493.9 3.2 fusion.14
  497.1 1.1 fusion.20
  498.2 9.8 %all-to-all-done.12 = bf16[8,128,256]{2,1,0:T(8,128)(2,1)S(1)} async-done(((bf16[8,128,256]{2,1,0:T(8,128)(2,1)}), bf16[8,128,256]{2,1,0:T(8,128)(2,1)S(1)}, u32[]{:S(2)}, u32[]{:S(2)}) %all-to-all-start.12) | async-done | bytes 524320 | tf_op jit(solution)/shard_map/all_to_all | solution.py:111
  (77 shorter events, 20.0 us)
Async XLA Ops:
  0.6 13.1 %copy-start = (bf16[1024,1024]{1,0:T(8,128)(2,1)S(1)}, bf16[1024,1024]{1,0:T(8,128)(2,1)}, u32[]{:S(2)}) copy-start(bf16[1024,1024]{1,0:T(8,128)(2,1)} %param.12) | copy-start | bytes 6291460
  0.7 3.8 copy-start.11
  7.4 18.7 %all-to-all-start = ((bf16[4,4,128,256]{2,3,0,1:T(8,128)(2,1)}), bf16[4,4,128,256]{2,3,0,1:T(8,128)(2,1)S(1)}, u32[]{:S(2)}, u32[]{:S(2)}) async-start(bf16[4,4,128,256]{2,3,0,1:T(8,128)(2,1)} %pad_maximum_fusion), calls=%async_computation | async-start | bytes 2097152 | tf_op jit(solution)/shard_map/all_to_all | solution.py:19
  26.1 1.0 copy-start.6
  27.0 54.4 %all-to-all-start.2 = ((bf16[8,128,1024]{2,1,0:T(8,128)(2,1)}), bf16[8,128,1024]{2,1,0:T(8,128)(2,1)S(1)}, u32[]{:S(2)}, u32[]{:S(2)}) async-start(bf16[8,128,1024]{2,1,0:T(8,128)(2,1)} %bitcast.139), calls=%async_computation.2 | async-start | bytes 4194304 | tf_op jit(solution)/shard_map/all_to_all | solution.py:65
  81.5 18.8 %all-to-all-start.9 = ((f32[2,4,128,256]{2,3,0,1:T(8,128)}), f32[2,4,128,256]{2,3,0,1:T(8,128)}, u32[]{:S(2)}, u32[]{:S(2)}) async-start(f32[2,4,128,256]{2,3,0,1:T(8,128)} %pad_maximum_fusion.1), calls=%async_computation.9 | async-start | bytes 2097152 | tf_op jit(solution)/shard_map/all_to_all | solution.py:19
  100.3 9.4 %all-to-all-start.3 = ((bf16[1,4,128,256]{3,2,0,1:T(8,128)(2,1)}), bf16[1,4,128,256]{3,2,0,1:T(8,128)(2,1)S(1)}, u32[]{:S(2)}, u32[]{:S(2)}) async-start(bf16[1,4,128,256]{3,2,0,1:T(8,128)(2,1)} %copy.133), calls=%async_computation.3 | async-start | bytes 524288 | tf_op jit(solution)/shard_map/all_to_all | solution.py:19
  104.4 6.8 %copy-start.7 = (bf16[1,128,4,256]{1,3,2,0:T(8,128)(2,1)}, bf16[1,128,4,256]{1,3,2,0:T(8,128)(2,1)S(1)}, u32[]{:S(2)}) copy-start(bf16[1,128,4,256]{1,3,2,0:T(8,128)(2,1)S(1)} %get-tuple-element.21) | copy-start | bytes 786436
  109.6 1.6 copy-start.13
  111.3 51.8 %all-to-all-start.1 = ((bf16[8,128,1024]{2,1,0:T(8,128)(2,1)}), bf16[8,128,1024]{2,1,0:T(8,128)(2,1)S(1)}, u32[]{:S(2)}, u32[]{:S(2)}) async-start(bf16[8,128,1024]{2,1,0:T(8,128)(2,1)} %stack.100), calls=%async_computation.1 | async-start | bytes 4194304 | tf_op jit(solution)/shard_map/all_to_all | solution.py:32
  163.0 2.0 copy-start.4
  165.0 52.0 %all-to-all-start.5 = ((bf16[8,128,1024]{2,1,0:T(8,128)(2,1)}), bf16[8,128,1024]{2,1,0:T(8,128)(2,1)S(1)}, u32[]{:S(2)}, u32[]{:S(2)}) async-start(bf16[8,128,1024]{2,1,0:T(8,128)(2,1)} %stack.102), calls=%async_computation.5 | async-start | bytes 4194304 | tf_op jit(solution)/shard_map/all_to_all | solution.py:32
  217.0 2.7 copy-start.2
  219.7 52.1 %all-to-all-start.4 = ((bf16[8,128,1024]{2,1,0:T(8,128)(2,1)}), bf16[8,128,1024]{2,1,0:T(8,128)(2,1)S(1)}, u32[]{:S(2)}, u32[]{:S(2)}) async-start(bf16[8,128,1024]{2,1,0:T(8,128)(2,1)} %stack.101), calls=%async_computation.4 | async-start | bytes 4194304 | tf_op jit(solution)/shard_map/all_to_all | solution.py:32
  271.8 10.7 %all-to-all-start.13 = ((f32[8,1,256]{2,1,0:T(1,128)}), f32[8,1,256]{2,1,0:T(1,128)S(1)}, u32[]{:S(2)}, u32[]{:S(2)}) async-start(f32[8,1,256]{2,1,0:T(1,128)} %bitcast.44), calls=%async_computation.13 | async-start | bytes 16384 | tf_op jit(solution)/shard_map/all_to_all | solution.py:114
  285.1 54.0 %all-to-all-start.10 = ((bf16[8,128,1024]{2,1,0:T(8,128)(2,1)}), bf16[8,128,1024]{2,1,0:T(8,128)(2,1)}, u32[]{:S(2)}, u32[]{:S(2)}) async-start(bf16[8,128,1024]{2,1,0:T(8,128)(2,1)} %stack.114), calls=%async_computation.10 | async-start | bytes 4194304 | tf_op jit(solution)/shard_map/all_to_all | solution.py:32
  293.4 1.7 copy-start.3
  340.7 4.5 copy-start.9
  340.7 52.3 %all-to-all-start.8 = ((bf16[8,128,1024]{2,1,0:T(8,128)(2,1)}), bf16[8,128,1024]{2,1,0:T(8,128)(2,1)}, u32[]{:S(2)}, u32[]{:S(2)}) async-start(bf16[8,128,1024]{2,1,0:T(8,128)(2,1)} %stack.109), calls=%async_computation.8 | async-start | bytes 4194304 | tf_op jit(solution)/shard_map/all_to_all | solution.py:32
  346.2 1.6 copy-start.5
  346.2 1.7 copy-start.10
  394.6 3.9 copy-start.15
  394.6 5.2 %copy-start.16 = (f32[256]{0:T(256)S(1)}, f32[256]{0:T(256)}, u32[]{:S(2)}) copy-start(f32[256]{0:T(256)} %param.23) | copy-start | bytes 3076
  394.6 5.2 %copy-start.17 = (f32[256]{0:T(256)S(1)}, f32[256]{0:T(256)}, u32[]{:S(2)}) copy-start(f32[256]{0:T(256)} %param.22) | copy-start | bytes 3076
  394.6 6.5 %copy-start.8 = (bf16[1,128,4,256]{1,3,2,0:T(8,128)(2,1)S(1)}, bf16[1,128,4,256]{1,3,2,0:T(8,128)(2,1)}, u32[]{:S(2)}) copy-start(bf16[1,128,4,256]{1,3,2,0:T(8,128)(2,1)} %copy-done.7) | copy-start | bytes 786436
  394.6 52.2 %all-to-all-start.7 = ((bf16[8,128,1024]{2,1,0:T(8,128)(2,1)}), bf16[8,128,1024]{2,1,0:T(8,128)(2,1)S(1)}, u32[]{:S(2)}, u32[]{:S(2)}) async-start(bf16[8,128,1024]{2,1,0:T(8,128)(2,1)} %stack.107), calls=%async_computation.7 | async-start | bytes 4194304 | tf_op jit(solution)/shard_map/all_to_all | solution.py:32
  446.9 10.6 %all-to-all-start.14 = ((f32[8,1,256]{2,1,0:T(1,128)}), f32[8,1,256]{2,1,0:T(1,128)S(1)}, u32[]{:S(2)}, u32[]{:S(2)}) async-start(f32[8,1,256]{2,1,0:T(1,128)} %broadcast_select_fusion), calls=%async_computation.14 | async-start | bytes 16384 | tf_op jit(solution)/shard_map/all_to_all | solution.py:121
  456.5 4.9 copy-start.12
  457.5 4.1 copy-start.14
  457.5 15.2 %all-to-all-start.11 = ((bf16[3,4,128,256]{3,2,0,1:T(8,128)(2,1)}), bf16[3,4,128,256]{3,2,0,1:T(8,128)(2,1)S(1)}, u32[]{:S(2)}, u32[]{:S(2)}) async-start(bf16[3,4,128,256]{3,2,0,1:T(8,128)(2,1)} %maximum_bitcast_fusion.1), calls=%async_computation.11 | async-start | bytes 1572864 | tf_op jit(solution)/shard_map/all_to_all | solution.py:27
  472.7 15.1 %all-to-all-start.6 = ((bf16[3,4,128,256]{3,2,0,1:T(8,128)(2,1)}), bf16[3,4,128,256]{3,2,0,1:T(8,128)(2,1)S(1)}, u32[]{:S(2)}, u32[]{:S(2)}) async-start(bf16[3,4,128,256]{3,2,0,1:T(8,128)(2,1)} %maximum_bitcast_fusion), calls=%async_computation.6 | async-start | bytes 1572864 | tf_op jit(solution)/shard_map/all_to_all | solution.py:27
  487.8 20.2 %all-to-all-start.12 = ((bf16[8,128,256]{2,1,0:T(8,128)(2,1)}), bf16[8,128,256]{2,1,0:T(8,128)(2,1)S(1)}, u32[]{:S(2)}, u32[]{:S(2)}) async-start(bf16[8,128,256]{2,1,0:T(8,128)(2,1)} %select_select_fusion), calls=%async_computation.12 | async-start | bytes 1048576 | tf_op jit(solution)/shard_map/all_to_all | solution.py:111
  493.9 15.5 %copy-start.1 = (bf16[1024,1024]{1,0:T(8,128)(2,1)S(1)}, bf16[1024,1024]{1,0:T(8,128)(2,1)}, u32[]{:S(2)}) copy-start(bf16[1024,1024]{1,0:T(8,128)(2,1)} %param.12) | copy-start | bytes 6291460
